TPU v7x, 256 devices: a whole 4x4x8 slice. The times are simulated.
256 devices in a mesh: rows: 32 (over z, x), cols: 8 (over y, core).
Axes of the slice: x: 4, y: 4, z: 8, core: 2. Of those that a mesh axis runs over, the one named last changes fastest.
Arguments:
- features: bfloat16 [524288, 440], P(('rows', 'cols')), may hold values from -12 to 12
- residual: float32 [524288, 147], P(('rows', 'cols')), may hold values from -6 to 6
- coeffs: float32 [524288, 147], P(('rows', 'cols')), may hold values from -3 to 3
- block_inverse: float32 [2, 2048, 2048], P(None, ('rows', 'cols')), may hold values from -0.0234375 to 0.0234375
- block_index: int32 [2, 2048], P(None, 'cols'), may hold values from 0 to 2047, as said below
- owners: int32 [2], replicated, may hold values from 0 to 31
Outputs:
- new_coeffs: float32 [524288, 147], P(('rows', 'cols'))
- new_residual: float32 [524288, 147], P(('rows', 'cols'))
Inputs may be any that keep to these rules, and one draw needn't show every extreme that they name: `block_index`: for each step and each aligned run of 256 positions, the indices are distinct.
All inputs are finite; a program needn't handle non-finite values.
Results may differ from a plain program's by a relative error of at most 0.0028.
Values may be sent and summed in bfloat16 or wider, within the bound.
A program may use at most 64 MiB of HBM per device.

v0:
```python
import jax
import jax.numpy as jnp
from jax import lax
from jax.sharding import Mesh
from jax.sharding import PartitionSpec as P

ROWS = ("rows_0", "rows_1")
COLS = ("cols_0", "cols_1")
ROWS_COLS = ("rows_0", "rows_1", "cols_0", "cols_1")
penalty = 0.5


def from_root(value, axes, root):
    value = jnp.where(lax.axis_index(axes) == root, value, jnp.zeros_like(value))
    for axis in axes:
        value = lax.psum(value, axis)
    return value


def in_order(parts, dim):
    shape = list(parts.shape[1:])
    shape[dim] *= parts.shape[0]
    return jnp.moveaxis(parts, 0, dim).reshape(shape)


def copy_for_each(value, axis):
    copies = jnp.broadcast_to(value, (lax.axis_size(axis), *value.shape))
    return lax.all_to_all(copies, axis, split_axis=0, concat_axis=0, tiled=True)


def collect(value, axis, dim):
    return in_order(copy_for_each(value, axis), dim)


def from_root_2(value, axis, root):
    return lax.dynamic_index_in_dim(lax.all_gather(value, axis), root, 0, keepdims=False)


def stacked_from(value, axes, order):
    parts = value[None]
    for k in order:
        parts = lax.all_gather(parts, axes[k], axis=0, tiled=True)
    block = [lax.axis_size(axes[k]) for k in reversed(order)]
    parts = parts.reshape(*block, *value.shape)
    turned = sorted(range(len(order)), key=lambda place: order[len(order) - 1 - place])
    return parts.transpose(*turned, *range(len(order), parts.ndim)).reshape(-1, *value.shape)


def gather_axes(value, axes, order, dim):
    return in_order(stacked_from(value, axes, order), dim)


def per_device(features, residual, coeffs, block_inverse, block_index, owners):
    frame_count = features.shape[0]
    feature_width = features.shape[1]
    per_col = block_index.shape[1]
    row_block = min(512, frame_count)
    exponent = -1.0 / feature_width
    my_row = lax.axis_index(ROWS)
    my_col = lax.axis_index(COLS)
    squares = jnp.sum(jnp.square(features.astype(jnp.float32)), axis=1)
    feature_blocks = features.reshape(frame_count // row_block, row_block, feature_width)
    norm_blocks = squares.reshape(frame_count // row_block, row_block)
    for step_id in range(block_index.shape[0]):
        chosen_rows = block_index[step_id]
        owner_row = owners[step_id]
        mine_feat = jnp.take(features, chosen_rows, axis=0)
        mine_res = jnp.take(residual, chosen_rows, axis=0)
        row_piece = from_root(mine_feat, ROWS, owner_row)
        chosen = collect(row_piece, COLS, 0)
        res_piece = from_root_2(mine_res, ROWS, owner_row)
        picked_res = collect(res_piece, COLS, 0)
        my_update = jnp.dot(
            block_inverse[step_id],
            picked_res,
            precision=lax.Precision.HIGHEST,
            preferred_element_type=jnp.float32,
        ).astype(jnp.bfloat16)
        update = gather_axes(my_update, ROWS_COLS, (1, 0, 2, 3), 0)
        chosen_norms = jnp.sum(jnp.square(chosen.astype(jnp.float32)), axis=1)

        def kernel_rows(operands):
            block_rows, block_norms = operands
            inner = lax.dot_general(
                block_rows, chosen, (((1,), (1,)), ((), ())), preferred_element_type=jnp.float32
            )
            distance = block_norms[:, None] + chosen_norms[None, :] - 2.0 * inner
            kernel = jnp.exp(distance * exponent).astype(jnp.bfloat16)
            return jnp.dot(kernel, update, preferred_element_type=jnp.float32)

        change = lax.map(kernel_rows, (feature_blocks, norm_blocks)).reshape(frame_count, -1)
        residual = residual - change
        is_owner = jnp.where(my_row == owner_row, 1.0, 0.0).astype(jnp.float32)
        mine_update = (
            lax.dynamic_slice_in_dim(update, my_col * per_col, per_col, 0).astype(jnp.float32)
            * is_owner
        )
        residual = residual.at[chosen_rows].add(-penalty * mine_update)
        coeffs = coeffs.at[chosen_rows].add(mine_update)
    return (coeffs, residual)


def solution(mesh):
    split = Mesh(mesh.devices.reshape(8, 4, 4, 2), ("rows_0", "rows_1", "cols_0", "cols_1"))
    in_specs = (
        P(ROWS_COLS, None),
        P(ROWS_COLS, None),
        P(ROWS_COLS, None),
        P(None, ROWS_COLS, None),
        P(None, COLS),
        P(),
    )
    out_specs = (P(ROWS_COLS, None), P(ROWS_COLS, None))
    return jax.shard_map(
        per_device, mesh=split, in_specs=in_specs, out_specs=out_specs, check_vma=False
    )
```

profile of v0, /device:TPU:1, one launch (start us, length us, event | category | flops | bytes accessed | tf_op | source)
XLA Modules:
  0.0 525.2 jit_solution(5898855721030536369)
XLA Ops:
  21.6 72.7 %all-reduce.5.cloned.1.call-done = (bf16[256,440]{1,0:T(8,128)(2,1)}, bf16[256,440]{1,0:T(8,128)(2,1)}) async-done(((bf16[256,440]{1,0:T(8,128)(2,1)}, bf16[256,440]{1,0:T(8,128)(2,1)}), (bf16[256,440]{1,0:T(8,128)(2,1)}, bf16[256,440]{1,0:T(8,128)(2,1)})) %all-reduce.5.cloned.1.call-update) | async-done | bytes 450576 | tf_op jit(solution)/shard_map/psum | solution.py:16
  97.1 49.7 %all-reduce.7.cloned.1.call-done = (bf16[256,440]{1,0:T(8,128)(2,1)}, bf16[256,440]{1,0:T(8,128)(2,1)}) async-done(((bf16[256,440]{1,0:T(8,128)(2,1)}, bf16[256,440]{1,0:T(8,128)(2,1)}), (bf16[256,440]{1,0:T(8,128)(2,1)}, bf16[256,440]{1,0:T(8,128)(2,1)})) %all-reduce.7.cloned.1.call-update) | async-done | bytes 450576 | tf_op jit(solution)/shard_map/psum | solution.py:16
  149.2 7.2 %all-to-all-start.1 = ((bf16[8,256,440]{1,2,0:T(8,128)(2,1)}), bf16[8,256,440]{1,2,0:T(8,128)(2,1)S(1)}, u32[]{:S(2)}, u32[]{:S(2)}) async-start(bf16[8,256,440]{1,2,0:T(8,128)(2,1)} %broadcast_in_dim.53), calls=%async_computation.1 | async-start | bytes 3604480 | tf_op jit(solution)/shard_map/all_to_all | solution.py:28
  158.1 40.6 %all-gather.7.cloned.1.call-done = f32[8192,147]{1,0:T(8,128)} async-done(((f32[256,147]{1,0:T(8,128)}), f32[8192,147]{1,0:T(8,128)}) %all-gather.7.cloned.1.call-update) | async-done | bytes 4816912 | tf_op jit(solution)/shard_map/all_gather | solution.py:36
  200.9 5.9 %all-to-all-start = ((f32[8,256,147]{1,2,0:T(8,128)}), f32[8,256,147]{1,2,0:T(8,128)S(1)}, u32[]{:S(2)}, u32[]{:S(2)}) async-start(f32[8,256,147]{1,2,0:T(8,128)} %broadcast_in_dim.51), calls=%async_computation | async-start | bytes 2490368 | tf_op jit(solution)/shard_map/all_to_all | solution.py:28
  211.8 12.0 %all-to-all-done = f32[8,256,147]{1,2,0:T(8,128)S(1)} async-done(((f32[8,256,147]{1,2,0:T(8,128)}), f32[8,256,147]{1,2,0:T(8,128)S(1)}, u32[]{:S(2)}, u32[]{:S(2)}) %all-to-all-start) | async-done | bytes 1204256 | tf_op jit(solution)/shard_map/all_to_all | solution.py:28
  226.2 9.1 %all-gather.1 = bf16[32,147]{1,0:T(8,128)(2,1)S(1)} all-gather(bf16[8,147]{1,0:T(8,128)(2,1)S(1)} %fusion.18), channel_id=3, replica_groups=mesh['rows_0'=8,'rows_1'=4,'cols_0'=4,'cols_1'=2] {'rows_1'}, dimensions={0}, use_global_device_ids=true | all-gather | bytes 11760 | tf_op jit(solution)/shard_map/all_gather | solution.py:42
  235.3 18.3 %all_gather.39 = bf16[32,8,147]{2,1,0:T(8,128)(2,1)S(1)} all-gather(bf16[4,8,147]{2,1,0:T(8,128)(2,1)S(1)} %bitcast.119), channel_id=1, replica_groups=mesh['rows_0'=8,'rows_1'=4,'cols_0'=4,'cols_1'=2] {'rows_0'}, dimensions={0}, use_global_device_ids=true | all-gather | bytes 84672 | tf_op jit(solution)/shard_map/all_gather | solution.py:42
  253.6 9.9 %all_gather.40 = bf16[128,8,147]{2,1,0:T(8,128)(2,1)S(1)} all-gather(bf16[32,8,147]{2,1,0:T(8,128)(2,1)S(1)} %all_gather.39), channel_id=1, replica_groups=mesh['rows_0'=8,'rows_1'=4,'cols_0'=4,'cols_1'=2] {'cols_0'}, dimensions={0}, use_global_device_ids=true | all-gather | bytes 376320 | tf_op jit(solution)/shard_map/all_gather | solution.py:42
  264.0 14.9 %all_gather.41 = bf16[256,8,147]{0,1,2:T(8,128)(2,1)S(1)} all-gather(bf16[128,8,147]{0,1,2:T(8,128)(2,1)S(1)} %copy.49), channel_id=1, replica_groups=mesh['rows_0'=8,'rows_1'=4,'cols_0'=4,'cols_1'=2] {'cols_1'}, dimensions={0}, use_global_device_ids=true | all-gather | bytes 903168 | tf_op jit(solution)/shard_map/all_gather | solution.py:42
  281.9 14.0 %while.20 = (s32[]{:T(128)}, f32[4,512,147]{1,2,0:T(8,128)S(1)}, f32[4,512]{1,0:T(4,128)S(1)}, f32[2048]{0:T(1024)S(1)}, bf16[4,512,440]{2,1,0:T(8,128)(2,1)}, /...) while((s32[]{:T(128)}, f32[4,512,147]{1,2,0:T(8,128)S(1)}, f32[4,512]{1,0:T(4,128)S(1)}, ...), condition=%wide.region_6.9_spmd, body=%wide.region_5.8_spmd.sunk | while | flops 1236271104 | bytes 3996769 | solution.py:91
  282.0 3.5 fusion.59
  285.5 3.5 fusion.59
  289.0 3.5 fusion.59
  292.5 3.5 fusion.59
  306.9 4.6 all-to-all-start.3
  313.6 84.1 %all-gather.9.cloned.1.call-done = f32[8192,147]{1,0:T(8,128)} async-done(((f32[256,147]{1,0:T(8,128)}), f32[8192,147]{1,0:T(8,128)}) %all-gather.9.cloned.1.call-update) | async-done | bytes 4816912 | tf_op jit(solution)/shard_map/all_gather | solution.py:36
  399.9 5.8 %all-to-all-start.2 = ((f32[8,256,147]{1,2,0:T(8,128)}), f32[8,256,147]{1,2,0:T(8,128)S(1)}, u32[]{:S(2)}, u32[]{:S(2)}) async-start(f32[8,256,147]{1,2,0:T(8,128)} %broadcast_in_dim.54), calls=%async_computation.2 | async-start | bytes 2490368 | tf_op jit(solution)/shard_map/all_to_all | solution.py:28
  410.3 3.8 copy.73
  414.1 5.1 scatter_custom_fusion
  419.1 3.6 all-to-all-done.2
  424.7 9.1 %all-gather.3 = bf16[32,147]{1,0:T(8,128)(2,1)S(1)} all-gather(bf16[8,147]{1,0:T(8,128)(2,1)S(1)} %fusion.19), channel_id=5, replica_groups=mesh['rows_0'=8,'rows_1'=4,'cols_0'=4,'cols_1'=2] {'rows_1'}, dimensions={0}, use_global_device_ids=true | all-gather | bytes 11760 | tf_op jit(solution)/shard_map/all_gather | solution.py:42
  433.8 18.3 %all_gather.45 = bf16[32,8,147]{2,1,0:T(8,128)(2,1)S(1)} all-gather(bf16[4,8,147]{2,1,0:T(8,128)(2,1)S(1)} %bitcast.120), channel_id=1, replica_groups=mesh['rows_0'=8,'rows_1'=4,'cols_0'=4,'cols_1'=2] {'rows_0'}, dimensions={0}, use_global_device_ids=true | all-gather | bytes 84672 | tf_op jit(solution)/shard_map/all_gather | solution.py:42
  452.1 9.9 %all_gather.46 = bf16[128,8,147]{2,1,0:T(8,128)(2,1)S(1)} all-gather(bf16[32,8,147]{2,1,0:T(8,128)(2,1)S(1)} %all_gather.45), channel_id=1, replica_groups=mesh['rows_0'=8,'rows_1'=4,'cols_0'=4,'cols_1'=2] {'cols_0'}, dimensions={0}, use_global_device_ids=true | all-gather | bytes 376320 | tf_op jit(solution)/shard_map/all_gather | solution.py:42
  462.5 15.1 %all_gather.47 = bf16[256,8,147]{0,1,2:T(8,128)(2,1)} all-gather(bf16[128,8,147]{0,1,2:T(8,128)(2,1)S(1)} %copy.62), channel_id=1, replica_groups=mesh['rows_0'=8,'rows_1'=4,'cols_0'=4,'cols_1'=2] {'cols_1'}, dimensions={0}, use_global_device_ids=true | all-gather | bytes 903168 | tf_op jit(solution)/shard_map/all_gather | solution.py:42
  480.6 5.1 scatter_custom_fusion.2
  488.4 16.6 %while.21 = (s32[]{:T(128)}, f32[4,512,147]{1,2,0:T(8,128)S(1)}, f32[4,512]{1,0:T(4,128)S(1)}, f32[2048]{0:T(1024)S(1)}, bf16[4,512,440]{2,1,0:T(8,128)(2,1)}, /...) while((s32[]{:T(128)}, f32[4,512,147]{1,2,0:T(8,128)S(1)}, f32[4,512]{1,0:T(4,128)S(1)}, ...), condition=%wide.region_13.16_spmd, body=%wide.region_12.15_spmd.sunk | while | flops 1236271104 | bytes 3996769 | solution.py:91
  488.5 4.1 fusion.63
  492.6 4.1 fusion.63
  496.8 4.1 fusion.63
  500.9 4.1 fusion.63
  510.0 5.1 scatter_custom_fusion.3
  (90 shorter events, 64.1 us)
Async XLA Ops:
  8.0 86.4 %all-reduce.5.cloned.1.call-start = ((), (), s32[]{:S(2)}) async-start(), calls=%async_computation.6 | async-start | bytes 1048576 | tf_op jit(solution)/shard_map/psum | solution.py:16
  14.3 3.7 copy-start.1
  16.2 78.3 %copy-start.3 = (f32[2048,147]{0,1:T(8,128)S(1)}, f32[2048,147]{0,1:T(8,128)}, u32[]{:S(2)}) copy-start(f32[2048,147]{0,1:T(8,128)} %param.15) | copy-start | bytes 3612676
  21.6 125.2 %all-reduce.7.cloned.1.call-start = ((), (), s32[]{:S(2)}) async-start(), calls=%async_computation.7 | async-start | bytes 1048576 | tf_op jit(solution)/shard_map/psum | solution.py:16
  94.4 104.3 %all-gather.7.cloned.1.call-start = ((), (), s32[]{:S(2)}) async-start(), calls=%async_computation.4 | async-start | bytes 8650752 | tf_op jit(solution)/shard_map/all_gather | solution.py:36
  95.3 53.9 %copy-start = (f32[2048,147]{1,0:T(8,128)}, f32[2048,147]{1,0:T(8,128)S(1)}, u32[]{:S(2)}) copy-start(f32[2048,147]{1,0:T(8,128)S(1)} %copy.46) | copy-start | bytes 3612676
  149.2 50.6 %all-to-all-start.1 = ((bf16[8,256,440]{1,2,0:T(8,128)(2,1)}), bf16[8,256,440]{1,2,0:T(8,128)(2,1)S(1)}, u32[]{:S(2)}, u32[]{:S(2)}) async-start(bf16[8,256,440]{1,2,0:T(8,128)(2,1)} %broadcast_in_dim.53), calls=%async_computation.1 | async-start | bytes 3604480 | tf_op jit(solution)/shard_map/all_to_all | solution.py:28
  200.9 7.8 %copy-start.6 = (s32[2,256]{1,0:T(2,128)S(1)}, s32[2,256]{1,0:T(2,128)}, u32[]{:S(2)}) copy-start(s32[2,256]{1,0:T(2,128)} %param.18) | copy-start | bytes 6148
  200.9 23.0 %all-to-all-start = ((f32[8,256,147]{1,2,0:T(8,128)}), f32[8,256,147]{1,2,0:T(8,128)S(1)}, u32[]{:S(2)}, u32[]{:S(2)}) async-start(f32[8,256,147]{1,2,0:T(8,128)} %broadcast_in_dim.51), calls=%async_computation | async-start | bytes 2490368 | tf_op jit(solution)/shard_map/all_to_all | solution.py:28
  206.8 190.9 %all-gather.9.cloned.1.call-start = ((), (), s32[]{:S(2)}) async-start(), calls=%async_computation.5 | async-start | bytes 8650752 | tf_op jit(solution)/shard_map/all_gather | solution.py:36
  224.2 0.9 copy-start.5
  280.0 2.0 copy-start.2
  303.6 1.8 copy-start.4
  306.9 91.8 %all-to-all-start.3 = ((bf16[8,256,440]{1,2,0:T(8,128)(2,1)}), bf16[8,256,440]{1,2,0:T(8,128)(2,1)}, u32[]{:S(2)}, u32[]{:S(2)}) async-start(bf16[8,256,440]{1,2,0:T(8,128)(2,1)} %broadcast_in_dim.56), calls=%async_computation.3 | async-start | bytes 3604480 | tf_op jit(solution)/shard_map/all_to_all | solution.py:28
  399.9 22.8 %all-to-all-start.2 = ((f32[8,256,147]{1,2,0:T(8,128)}), f32[8,256,147]{1,2,0:T(8,128)S(1)}, u32[]{:S(2)}, u32[]{:S(2)}) async-start(f32[8,256,147]{1,2,0:T(8,128)} %broadcast_in_dim.54), calls=%async_computation.2 | async-start | bytes 2490368 | tf_op jit(solution)/shard_map/all_to_all | solution.py:28
Sparse Core Ops, SparseCore 0:
  21.7 72.6 all-reduce.4
  96.8 49.8 all-reduce.6
Sparse Core Ops, SparseCore 1:
  98.0 100.6 all-gather.6
  305.5 92.2 all-gather.8
where the time goes:
time: 527 us; the launch traced here: 525 us
  waiting for transfers between devices  263 us (50%)
  blocking collectives  105 us (20%)
  local copies, waits for them, and re-layouts  47.4 us (9%)
  other arithmetic  33.4 us (6%)
  matrix products  32.5 us (6%)
  starting transfers between devices  23.5 us (4%)
  between operations  20.9 us (4%)
    all_gather x2, waiting for transfers between devices, from_root_2(): lax.all_gather(value, axis)  125 us
    psum x2, waiting for transfers between devices, from_root(): value = lax.psum(value, axis)  122 us
    all_gather x8, blocking collectives, stacked_from(): parts = lax.all_gather(parts, axes[k], axis=0, tiled=True)  105 us
    dot_general x8, matrix products, kernel_rows(): return jnp.dot(kernel, update, preferred_element_type=jnp.float32)  30.4 us
    all_to_all x4, starting transfers between devices, copy_for_each(): return lax.all_to_all(copies, axis, split_axis=0, concat_axis=0, tiled=True)  23.4 us
    all_to_all x4, waiting for transfers between devices, copy_for_each(): return lax.all_to_all(copies, axis, split_axis=0, concat_axis=0, tiled=True)  15.6 us
    unnamed x27, local copies, waits for them, and re-layouts  14.1 us
  transfers between devices with their start and end apart: 8, of which 6 were waited for; matrix products, arithmetic and copies ran while one was open for 5% of the time, Pallas kernels for 0%

commit v1 on v0

--- a/solution.py
+++ b/solution.py
@@ -13,7 +13,7 @@
 def from_root(value, axes, root):
     value = jnp.where(lax.axis_index(axes) == root, value, jnp.zeros_like(value))
     for axis in axes:
-        value = lax.psum(value, axis)
+        value = jnp.sum(lax.all_gather(value, axis), axis=0)
     return value
 
 

time: 527 us -> 487 us (0.924)
  waiting for transfers between devices: 263 us -> 185 us
  blocking collectives: 105 us -> 131 us
  starting transfers between devices: 23.5 us -> 31.6 us
    psum x2 -> x0, waiting for transfers between devices: 122 us -> none  [from_root(): value = lax.psum(value, axis)]
    all_gather x0 -> x2, waiting for transfers between devices: none -> 37.9 us  [from_root(): value = jnp.sum(lax.all_gather(value, axis), axis=0)]
    all_gather x0 -> x2, blocking collectives: none -> 26 us  [from_root(): value = jnp.sum(lax.all_gather(value, axis), axis=0)]
    all_gather x2, waiting for transfers between devices: 125 us -> 139 us  [from_root_2(): lax.all_gather(value, axis)]
    all_to_all x4, starting transfers between devices: 23.4 us -> 31.5 us  [copy_for_each(): return lax.all_to_all(copies, axis, split_axis=0, concat_axis=0, tiled=True)]
    all_to_all x4, waiting for transfers between devices: 15.6 us -> 8.72 us  [copy_for_each(): return lax.all_to_all(copies, axis, split_axis=0, concat_axis=0, tiled=True)]
    unnamed x27 -> x31, local copies, waits for them, and re-layouts: 14.1 us -> 12.7 us
  transfers between devices with their start and end apart: 8 -> 8, of which waited for: 6 -> 5; matrix products, arithmetic and copies ran while one was open for 5% -> 14% of each run, Pallas kernels for 0% -> 0%
where the time goes in v1:
time: 487 us; the launch traced here: 486 us
  waiting for transfers between devices  185 us (38%)
  blocking collectives  131 us (27%)
  local copies, waits for them, and re-layouts  46.7 us (10%)
  other arithmetic  37.5 us (8%)
  matrix products  34.4 us (7%)
  starting transfers between devices  31.6 us (6%)
  between operations  19.2 us (4%)
    all_gather x2, waiting for transfers between devices, from_root_2(): lax.all_gather(value, axis)  139 us
    all_gather x8, blocking collectives, stacked_from(): parts = lax.all_gather(parts, axes[k], axis=0, tiled=True)  105 us
    all_gather x2, waiting for transfers between devices, from_root(): value = jnp.sum(lax.all_gather(value, axis), axis=0)  37.9 us
    dot_general x8, matrix products, kernel_rows(): return jnp.dot(kernel, update, preferred_element_type=jnp.float32)  32.3 us
    all_to_all x4, starting transfers between devices, copy_for_each(): return lax.all_to_all(copies, axis, split_axis=0, concat_axis=0, tiled=True)  31.5 us
    all_gather x2, blocking collectives, from_root(): value = jnp.sum(lax.all_gather(value, axis), axis=0)  26 us
    unnamed x31, local copies, waits for them, and re-layouts  12.7 us
    while x4, local copies, waits for them, and re-layouts, per_device(): lax.map(kernel_rows, (feature_blocks, norm_blocks)).reshape(frame_count, -1)  11.2 us
  transfers between devices with their start and end apart: 8, of which 5 were waited for; matrix products, arithmetic and copies ran while one was open for 14% of the time, Pallas kernels for 0%

profile of v1, /device:TPU:1, one launch (start us, length us, event | category | flops | bytes accessed | tf_op | source)
XLA Modules:
  0.0 486.1 jit_solution(17419542322727183345)
XLA Ops:
  19.3 37.9 %all-gather.15.cloned.1.call-done = bf16[2048,440]{1,0:T(8,128)(2,1)} async-done(((bf16[256,440]{1,0:T(8,128)(2,1)}), bf16[2048,440]{1,0:T(8,128)(2,1)}) %all-gather.15.cloned.1.call-update) | async-done | bytes 1802256 | tf_op jit(solution)/shard_map/all_gather | solution.py:16
  59.2 12.9 %all-gather.3 = bf16[1024,440]{1,0:T(8,128)(2,1)S(1)} all-gather(bf16[256,440]{1,0:T(8,128)(2,1)S(1)} %reduce_sum.80), channel_id=5, replica_groups=mesh['rows_0'=8,'rows_1'=4,'cols_0'=4,'cols_1'=2] {'rows_1'}, dimensions={0}, use_global_device_ids=true | all-gather | bytes 1126400 | tf_op jit(solution)/shard_map/all_gather | solution.py:16
  73.9 11.7 %all-to-all-start.1 = ((bf16[8,256,440]{1,2,0:T(8,128)(2,1)}), bf16[8,256,440]{1,2,0:T(8,128)(2,1)}, u32[]{:S(2)}, u32[]{:S(2)}) async-start(bf16[8,256,440]{1,2,0:T(8,128)(2,1)} %broadcast_in_dim.53), calls=%async_computation.1 | async-start | bytes 3604480 | tf_op jit(solution)/shard_map/all_to_all | solution.py:28
  87.5 72.9 %all-gather.13.cloned.1.call-done = f32[8192,147]{1,0:T(8,128)} async-done(((f32[256,147]{1,0:T(8,128)}), f32[8192,147]{1,0:T(8,128)}) %all-gather.13.cloned.1.call-update) | async-done | bytes 4816912 | tf_op jit(solution)/shard_map/all_gather | solution.py:36
  162.6 5.7 %all-to-all-start = ((f32[8,256,147]{1,2,0:T(8,128)}), f32[8,256,147]{1,2,0:T(8,128)S(1)}, u32[]{:S(2)}, u32[]{:S(2)}) async-start(f32[8,256,147]{1,2,0:T(8,128)} %broadcast_in_dim.51), calls=%async_computation | async-start | bytes 2490368 | tf_op jit(solution)/shard_map/all_to_all | solution.py:28
  176.4 3.8 copy.148
  180.2 5.1 %all-to-all-done = f32[8,256,147]{1,2,0:T(8,128)S(1)} async-done(((f32[8,256,147]{1,2,0:T(8,128)}), f32[8,256,147]{1,2,0:T(8,128)S(1)}, u32[]{:S(2)}, u32[]{:S(2)}) %all-to-all-start) | async-done | bytes 1204256 | tf_op jit(solution)/shard_map/all_to_all | solution.py:28
  187.7 9.8 %all-gather.1 = bf16[32,147]{1,0:T(8,128)(2,1)S(1)} all-gather(bf16[8,147]{1,0:T(8,128)(2,1)S(1)} %fusion.18), channel_id=3, replica_groups=mesh['rows_0'=8,'rows_1'=4,'cols_0'=4,'cols_1'=2] {'rows_1'}, dimensions={0}, use_global_device_ids=true | all-gather | bytes 11760 | tf_op jit(solution)/shard_map/all_gather | solution.py:42
  197.5 19.8 %all_gather.63 = bf16[32,8,147]{2,1,0:T(8,128)(2,1)S(1)} all-gather(bf16[4,8,147]{2,1,0:T(8,128)(2,1)S(1)} %bitcast.127), channel_id=1, replica_groups=mesh['rows_0'=8,'rows_1'=4,'cols_0'=4,'cols_1'=2] {'rows_0'}, dimensions={0}, use_global_device_ids=true | all-gather | bytes 84672 | tf_op jit(solution)/shard_map/all_gather | solution.py:42
  217.2 10.2 %all_gather.64 = bf16[128,8,147]{2,1,0:T(8,128)(2,1)S(1)} all-gather(bf16[32,8,147]{2,1,0:T(8,128)(2,1)S(1)} %all_gather.63), channel_id=1, replica_groups=mesh['rows_0'=8,'rows_1'=4,'cols_0'=4,'cols_1'=2] {'cols_0'}, dimensions={0}, use_global_device_ids=true | all-gather | bytes 376320 | tf_op jit(solution)/shard_map/all_gather | solution.py:42
  227.9 12.7 %all_gather.65 = bf16[256,8,147]{0,1,2:T(8,128)(2,1)} all-gather(bf16[128,8,147]{0,1,2:T(8,128)(2,1)S(1)} %copy.121), channel_id=1, replica_groups=mesh['rows_0'=8,'rows_1'=4,'cols_0'=4,'cols_1'=2] {'cols_1'}, dimensions={0}, use_global_device_ids=true | all-gather | bytes 903168 | tf_op jit(solution)/shard_map/all_gather | solution.py:42
  243.8 15.9 %while.20 = (s32[]{:T(128)}, f32[4,512,147]{1,2,0:T(8,128)S(1)}, f32[4,512]{1,0:T(4,128)S(1)}, f32[2048]{0:T(1024)S(1)}, bf16[4,512,440]{2,1,0:T(8,128)(2,1)S(1)...) while((s32[]{:T(128)}, f32[4,512,147]{1,2,0:T(8,128)S(1)}, f32[4,512]{1,0:T(4,128)S(1)}, ...), condition=%wide.region_6.9_spmd, body=%wide.region_5.8_spmd.sunk | while | flops 1236271104 | bytes 3996761 | solution.py:91
  243.8 3.9 fusion.59
  247.8 4.0 fusion.59
  251.8 4.0 fusion.59
  255.8 4.0 fusion.59
  271.2 13.1 %all-gather.7 = bf16[1024,440]{1,0:T(8,128)(2,1)S(1)} all-gather(bf16[256,440]{1,0:T(8,128)(2,1)S(1)} %reduce_sum.84), channel_id=9, replica_groups=mesh['rows_0'=8,'rows_1'=4,'cols_0'=4,'cols_1'=2] {'rows_1'}, dimensions={0}, use_global_device_ids=true | all-gather | bytes 1126400 | tf_op jit(solution)/shard_map/all_gather | solution.py:16
  286.1 8.4 %all-to-all-start.3 = ((bf16[8,256,440]{1,2,0:T(8,128)(2,1)}), bf16[8,256,440]{1,2,0:T(8,128)(2,1)}, u32[]{:S(2)}, u32[]{:S(2)}) async-start(bf16[8,256,440]{1,2,0:T(8,128)(2,1)} %broadcast_in_dim.56), calls=%async_computation.3 | async-start | bytes 3604480 | tf_op jit(solution)/shard_map/all_to_all | solution.py:28
  296.3 65.9 %all-gather.17.cloned.1.call-done = f32[8192,147]{1,0:T(8,128)} async-done(((f32[256,147]{1,0:T(8,128)}), f32[8192,147]{1,0:T(8,128)}) %all-gather.17.cloned.1.call-update) | async-done | bytes 4816912 | tf_op jit(solution)/shard_map/all_gather | solution.py:36
  364.4 5.7 %all-to-all-start.2 = ((f32[8,256,147]{1,2,0:T(8,128)}), f32[8,256,147]{1,2,0:T(8,128)S(1)}, u32[]{:S(2)}, u32[]{:S(2)}) async-start(f32[8,256,147]{1,2,0:T(8,128)} %broadcast_in_dim.54), calls=%async_computation.2 | async-start | bytes 2490368 | tf_op jit(solution)/shard_map/all_to_all | solution.py:28
  374.7 3.8 copy.151
  378.5 5.0 %scatter_custom_fusion = f32[2048,147]{1,0:T(8,128)} fusion(f32[2048,147]{1,0:T(8,128)} %copy.124, s32[256]{0:T(256)} %bitcast.144, f32[]{:T(128)S(6)} %select_n.70, bf16[2048,147]{1,0:T(8,128)(2,1)} %get-tuple-element.337, s32[]{:T(128)S(6)} %select_n.69, s32[]{:T(128)} %constant.60.clone.1), kind=kCustom, calls=%fused_computation.46 | custom fusion | flops 112896 | bytes 1335816 | tf_op jit(solution)/shard_map/scatter-add | solution.py:99
  389.1 9.1 %all-gather.5 = bf16[32,147]{1,0:T(8,128)(2,1)S(1)} all-gather(bf16[8,147]{1,0:T(8,128)(2,1)S(1)} %fusion.19), channel_id=7, replica_groups=mesh['rows_0'=8,'rows_1'=4,'cols_0'=4,'cols_1'=2] {'rows_1'}, dimensions={0}, use_global_device_ids=true | all-gather | bytes 11760 | tf_op jit(solution)/shard_map/all_gather | solution.py:42
  398.3 18.3 %all_gather.73 = bf16[32,8,147]{2,1,0:T(8,128)(2,1)S(1)} all-gather(bf16[4,8,147]{2,1,0:T(8,128)(2,1)S(1)} %bitcast.128), channel_id=1, replica_groups=mesh['rows_0'=8,'rows_1'=4,'cols_0'=4,'cols_1'=2] {'rows_0'}, dimensions={0}, use_global_device_ids=true | all-gather | bytes 84672 | tf_op jit(solution)/shard_map/all_gather | solution.py:42
  416.6 9.9 %all_gather.74 = bf16[128,8,147]{2,1,0:T(8,128)(2,1)S(1)} all-gather(bf16[32,8,147]{2,1,0:T(8,128)(2,1)S(1)} %all_gather.73), channel_id=1, replica_groups=mesh['rows_0'=8,'rows_1'=4,'cols_0'=4,'cols_1'=2] {'cols_0'}, dimensions={0}, use_global_device_ids=true | all-gather | bytes 376320 | tf_op jit(solution)/shard_map/all_gather | solution.py:42
  426.9 15.3 %all_gather.75 = bf16[256,8,147]{0,1,2:T(8,128)(2,1)} all-gather(bf16[128,8,147]{0,1,2:T(8,128)(2,1)S(1)} %copy.135), channel_id=1, replica_groups=mesh['rows_0'=8,'rows_1'=4,'cols_0'=4,'cols_1'=2] {'cols_1'}, dimensions={0}, use_global_device_ids=true | all-gather | bytes 903168 | tf_op jit(solution)/shard_map/all_gather | solution.py:42
  445.4 16.6 %while.21 = (s32[]{:T(128)}, f32[4,512,147]{1,2,0:T(8,128)S(1)}, f32[4,512]{1,0:T(4,128)S(1)}, f32[2048]{0:T(1024)S(1)}, bf16[4,512,440]{2,1,0:T(8,128)(2,1)}, /...) while((s32[]{:T(128)}, f32[4,512,147]{1,2,0:T(8,128)S(1)}, f32[4,512]{1,0:T(4,128)S(1)}, ...), condition=%wide.region_13.16_spmd, body=%wide.region_12.15_spmd.sunk | while | flops 1236271104 | bytes 3996761 | solution.py:91
  445.4 4.1 fusion.63
  449.5 4.1 fusion.63
  453.7 4.1 fusion.63
  457.8 4.1 fusion.63
  467.0 5.1 %scatter_custom_fusion.3 = f32[2048,147]{1,0:T(8,128)} fusion(f32[2048,147]{1,0:T(8,128)} %bitcast_subtract_fusion, s32[256]{0:T(256)S(1)} %bitcast.141, f32[]{:T(128)S(6)} %select_n.75, f32[]{:T(128)} %constant.94.clone.1, bf16[2048,147]{1,0:T(8,128)(2,1)} %get-tuple-element.338, s32[]{:T(128)S(6)} %select_n.69, s32[]{:T(128)} %constant.60.clone.1), kind=kCustom, calls=%fused_computation.39 | custom fusion | flops 150528 | bytes 1336328 | tf_op jit(solution)/shard_map/scatter-add | solution.py:98
  (98 shorter events, 72.4 us)
Async XLA Ops:
  7.2 50.0 %all-gather.15.cloned.1.call-start = ((), (), s32[]{:S(2)}) async-start(), calls=%async_computation.5 | async-start | bytes 2359296 | tf_op jit(solution)/shard_map/all_gather | solution.py:16
  12.2 4.4 copy-start.1
  12.2 4.5 copy-start.4
  16.6 143.8 %all-gather.13.cloned.1.call-start = ((), (), s32[]{:S(2)}) async-start(), calls=%async_computation.4 | async-start | bytes 8650752 | tf_op jit(solution)/shard_map/all_gather | solution.py:36
  17.4 41.7 %copy-start = (f32[2048,147]{1,0:T(8,128)}, f32[2048,147]{1,0:T(8,128)S(1)}, u32[]{:S(2)}) copy-start(f32[2048,147]{1,0:T(8,128)S(1)} %copy.118) | copy-start | bytes 3612676
  73.9 87.6 %all-to-all-start.1 = ((bf16[8,256,440]{1,2,0:T(8,128)(2,1)}), bf16[8,256,440]{1,2,0:T(8,128)(2,1)}, u32[]{:S(2)}, u32[]{:S(2)}) async-start(bf16[8,256,440]{1,2,0:T(8,128)(2,1)} %broadcast_in_dim.53), calls=%async_computation.1 | async-start | bytes 3604480 | tf_op jit(solution)/shard_map/all_to_all | solution.py:28
  161.3 7.6 %copy-start.2 = (bf16[2048,440]{1,0:T(8,128)(2,1)S(1)}, bf16[2048,440]{1,0:T(8,128)(2,1)}, u32[]{:S(2)}) copy-start(bf16[2048,440]{1,0:T(8,128)(2,1)} %copy-done.1) | copy-start | bytes 5406724
  162.6 22.8 %all-to-all-start = ((f32[8,256,147]{1,2,0:T(8,128)}), f32[8,256,147]{1,2,0:T(8,128)S(1)}, u32[]{:S(2)}, u32[]{:S(2)}) async-start(f32[8,256,147]{1,2,0:T(8,128)} %broadcast_in_dim.51), calls=%async_computation | async-start | bytes 2490368 | tf_op jit(solution)/shard_map/all_to_all | solution.py:28
  168.3 100.9 %all-gather.19.cloned.1.call-start = ((), (), s32[]{:S(2)}) async-start(), calls=%async_computation.7 | async-start | bytes 2359296 | tf_op jit(solution)/shard_map/all_gather | solution.py:16
  168.9 5.6 %copy-start.6 = (s32[2,256]{1,0:T(2,128)S(1)}, s32[2,256]{1,0:T(2,128)}, u32[]{:S(2)}) copy-start(s32[2,256]{1,0:T(2,128)} %param.18) | copy-start | bytes 6148
  172.6 189.6 %all-gather.17.cloned.1.call-start = ((), (), s32[]{:S(2)}) async-start(), calls=%async_computation.6 | async-start | bytes 8650752 | tf_op jit(solution)/shard_map/all_gather | solution.py:36
  174.5 89.5 %copy-start.7 = (s32[256,1]{0,1:T(1,128)}, s32[256,1]{0,1:T(1,128)S(1)}, u32[]{:S(2)}) copy-start(s32[256,1]{0,1:T(1,128)S(1)} %get-tuple-element.181) | copy-start | bytes 3076
  185.7 0.9 copy-start.5
  286.1 77.2 %all-to-all-start.3 = ((bf16[8,256,440]{1,2,0:T(8,128)(2,1)}), bf16[8,256,440]{1,2,0:T(8,128)(2,1)}, u32[]{:S(2)}, u32[]{:S(2)}) async-start(bf16[8,256,440]{1,2,0:T(8,128)(2,1)} %broadcast_in_dim.56), calls=%async_computation.3 | async-start | bytes 3604480 | tf_op jit(solution)/shard_map/all_to_all | solution.py:28
  364.4 22.8 %all-to-all-start.2 = ((f32[8,256,147]{1,2,0:T(8,128)}), f32[8,256,147]{1,2,0:T(8,128)S(1)}, u32[]{:S(2)}, u32[]{:S(2)}) async-start(f32[8,256,147]{1,2,0:T(8,128)} %broadcast_in_dim.54), calls=%async_computation.2 | async-start | bytes 2490368 | tf_op jit(solution)/shard_map/all_to_all | solution.py:28
  472.0 2.8 copy-start.3
Sparse Core Ops, SparseCore 0:
  16.7 40.4 all-gather.14
  60.3 99.9 all-gather.12
  172.7 33.8 all-gather.18
  269.3 92.8 all-gather.16
